TPU v7x, 32 devices: a whole 2x2x4 slice. The times are simulated.
32 devices in a mesh: prow: 4 (over z), pcol: 8 (over y, x, core).
Axes of the slice: x: 2, y: 2, z: 4, core: 2. Of those that a mesh axis runs over, the one named last changes fastest.
Arguments:
- site_code: int32 [17408], P(('prow', 'pcol')), may hold values from 0 to 285212671, as said below
- length_scale: float32 [1], replicated, may hold values from 6 to 12
- noise_var: float32 [1], replicated, may hold values from 0.3 to 1
Outputs:
- panel: bfloat16 [16, 1024, 1024], P('prow')
- trailing: bfloat16 [16, 1024, 8, 1024], P('prow', None, 'pcol')
Inputs may be any that keep to these rules, and one draw needn't show every extreme that they name: `site_code`: each entry is 128 * 128 * s + 128 * x + y for a slot s and bins x, y in 0 .. 127; every slot of 0 .. 17407 appears once. With b = s // 1024 and r = s mod 1024, the home of slot s is the device of prow-major index r mod (32) if b = 0, else the device (prow (b - 1) mod 4, pcol r mod 8); no device holds more than 17 sites of one home, and some device holds exactly 17 sites of some home.
All inputs are finite; a program needn't handle non-finite values.
Results may differ from a plain program's by a relative error of at most 0.0036.
Values may be sent and summed in bfloat16 or wider, within the bound.
No kernel may reach another device: no remote copies, remote signals or barrier semaphores. Data moves between devices by JAX's collectives and lax.ppermute only.
A program may use at most 192 MiB of HBM per device.

v0:
```python
import jax
import jax.numpy as jnp
from jax import lax
from jax.sharding import PartitionSpec as P

B = 1024
GRID = 128
TR_DEV = 4
SLAB_DEV = 1


def from_root(value, axis, source):
    kept = jnp.where(lax.axis_index(axis) == source, value, 0).astype(value.dtype)
    return lax.psum(kept, axis)


def site_features(codes):
    coord_x = (codes // GRID % GRID).astype(jnp.float32)
    coord_y = (codes % GRID).astype(jnp.float32)
    radius_sq = coord_x * coord_x + coord_y * coord_y
    ones = jnp.ones_like(coord_x)
    left = jnp.stack([coord_x, coord_y, radius_sq, ones], -2)
    right = jnp.stack([-2.0 * coord_x, -2.0 * coord_y, ones, radius_sq], -2)
    return (left, right)


def cov_tile(left, right, decay_rate, nugget, same):
    squared = jnp.einsum("...ka,kb->...ab", left, right, precision=lax.Precision.HIGHEST)
    distance = jnp.sqrt(jnp.maximum(squared, 0.0))
    scaled = decay_rate * distance
    values = (1.0 + scaled) * jnp.exp(-scaled)
    rank_count = values.ndim
    eye_mask = lax.broadcasted_iota(
        jnp.int32, values.shape, rank_count - 2
    ) == lax.broadcasted_iota(jnp.int32, values.shape, rank_count - 1)
    return values + jnp.where(eye_mask, nugget * same, 0.0)


def body(site_code, length_scale, noise_var):
    n_prow = lax.axis_size("prow")
    n_pcol = lax.axis_size("pcol")
    devices = n_prow * n_pcol
    me_row = lax.axis_index("prow")
    me_col = lax.axis_index("pcol")
    decay_rate = jnp.sqrt(3.0) / length_scale[0]
    nugget = noise_var[0]
    pick_index = me_col // n_prow + jnp.arange(SLAB_DEV, dtype=jnp.int32) * (n_pcol // n_prow)
    capacity = (TR_DEV * B // n_pcol + B // devices + devices - 1) // devices
    site_slot = site_code // (GRID * GRID)
    block_id = site_slot // B
    block_pos = site_slot % B
    home_dev = jnp.where(
        block_id == 0, block_pos % devices, (block_id - 1) % n_prow * n_pcol + block_pos % n_pcol
    )
    one_hot = (home_dev[:, None] == jnp.arange(devices, dtype=jnp.int32)[None, :]).astype(jnp.int32)
    arrival_rank = jnp.sum(jnp.cumsum(one_hot, axis=0) * one_hot, axis=1) - 1
    outbox = jnp.full((devices, capacity), -1, jnp.int32).at[home_dev, arrival_rank].set(site_code)
    inbox = lax.all_to_all(
        outbox, ("prow", "pcol"), split_axis=0, concat_axis=0, tiled=True
    ).reshape(-1)
    valid = inbox >= 0
    got_slot = jnp.where(valid, inbox // (GRID * GRID), 0)
    got_block = got_slot // B
    got_pos = got_slot % B
    row_width = B // n_pcol
    tile_index = jnp.where(valid & (got_block > 0), (got_block - 1) // n_prow, TR_DEV)
    row_home = (
        jnp.full((TR_DEV, row_width), -1, jnp.int32)
        .at[tile_index, got_pos // n_pcol]
        .set(inbox, mode="drop")
    )
    panel_width = B // devices
    panel_index = jnp.where(valid & (got_block == 0), got_pos // devices, panel_width)
    panel_home = jnp.full((panel_width,), -1, jnp.int32).at[panel_index].set(inbox, mode="drop")
    row_all = lax.all_gather(row_home, "pcol", axis=1, tiled=True)
    row_codes = row_all.reshape(TR_DEV, n_pcol, row_width).transpose(0, 2, 1).reshape(TR_DEV, B)
    panel_all = lax.all_gather(panel_home, ("prow", "pcol"), axis=0, tiled=True)
    panel_codes = panel_all.reshape(devices, panel_width).T.reshape(B)
    col_codes = from_root(jnp.take(row_codes, pick_index, axis=0), "prow", me_col % n_prow)
    panel_left, panel_right = site_features(panel_codes)
    row_left, row_right = site_features(row_codes)
    col_left, col_right = site_features(col_codes)

    def factor_panel(unused):
        diag_factor = jnp.linalg.cholesky(
            cov_tile(panel_left, panel_right, decay_rate, nugget, 1.0)
        )
        tiles = cov_tile(row_left, panel_right, decay_rate, nugget, 0.0)
        solved = jax.scipy.linalg.solve_triangular(
            diag_factor, tiles.reshape(TR_DEV * B, B).T, lower=True
        )
        return solved.T.reshape(TR_DEV, B, B).astype(jnp.bfloat16)

    def skip_panel(unused):
        return jnp.zeros((TR_DEV, B, B), jnp.bfloat16)

    panel_mine = lax.cond(me_col == 0, factor_panel, skip_panel, 0)
    panel_rows = from_root(panel_mine, "pcol", 0)
    panel_pick = jnp.take(panel_rows, pick_index, axis=0)
    panel_cols = from_root(panel_pick, "prow", me_col % n_prow)
    row_results = []
    for row_tile in range(TR_DEV):
        trail = row_tile * n_prow + me_row
        other = 0 + me_col
        same = jnp.where(trail == other, 1.0, 0.0)
        tile = cov_tile(row_left[row_tile], col_right[0], decay_rate, nugget, same)
        product = lax.dot_general(
            panel_rows[row_tile],
            panel_cols[0],
            (((1,), (1,)), ((), ())),
            preferred_element_type=jnp.float32,
        )
        col_results = [(tile - product).astype(jnp.bfloat16)]
        row_results.append(jnp.stack(col_results, 1))
    trailing = jnp.stack(row_results, 0)
    return (panel_rows, trailing)


def solution(mesh):
    in_specs = (P(("prow", "pcol")), P(), P())
    out_specs = (P("prow", None, None), P("prow", None, "pcol", None))
    return jax.shard_map(body, mesh=mesh, in_specs=in_specs, out_specs=out_specs, check_vma=False)
```

profile of v0, /device:TPU:0, one launch (start us, length us, event | category | flops | bytes accessed | tf_op | source)
XLA Modules:
  0.0 914.7 jit_solution(17226715184799600394)
XLA Ops:
  9.8 46.5 %scatter_fusion = s32[32,17]{0,1:T(8,128)S(1)} fusion(s32[32,17]{0,1:T(8,128)S(1)} %broadcast_in_dim.85, s32[544]{0:T(1024)S(1)} %fusion.113, s32[544]{0:T(1024)} %param.5), kind=kCustom, calls=%fused_computation | custom fusion | bytes 10880 | tf_op jit(solution)/shard_map/scatter | solution.py:57
  73.1 25.6 %scatter_fusion.1 = s32[4,128]{1,0:T(4,128)S(1)} fusion(s32[4,128]{1,0:T(4,128)S(1)} %broadcast_in_dim.87, s32[544]{0:T(1024)S(1)} %get-tuple-element.66, s32[544]{0:T(1024)S(1)} %reshape.975), kind=kCustom, calls=%fused_computation.2 | custom fusion | bytes 10880 | tf_op jit(solution)/shard_map/scatter | solution.py:70
  98.7 8.0 all_gather.7
  111.4 38.2 %all-reduce.2 = s32[1024]{0:T(1024)S(1)} all-reduce(s32[1024]{0:T(1024)S(1)} %dynamic-update-slice.49), channel_id=1, replica_groups=mesh['prow'=4,'pcol'=8] {'prow','pcol'}, use_global_device_ids=true, to_apply=%add.2 | all-reduce | flops 1024 | bytes 8192
  150.1 487.0 %conditional.1 = (bf16[4,1024,1024]{2,1,0:T(8,128)(2,1)}) conditional(s32[]{:T(128)} %convert_element_type.98, () %tuple.14, (f32[]{:T(128)}, f32[4,1024]{1,0:T(4,128)S(1)}, f32[4,1024]{1,0:T(4,128)S(1)}, f32[]{:T(128)}, f32[4,4,1024]{2,0,1:T(4,128)S(1)}) %tuple.15), branch_computations={%region_6.7_spmd, %region_7.24_spmd} | conditional | flops 32137316352 | bytes 414441856 | solution.py:97
  173.7 11.7 %cholesky.5 = f32[128,128]{1,0:T(8,128)S(1)} custom-call(f32[128,128]{1,0:T(8,128)S(1)} %cholesky.221), custom_call_target="Cholesky" | custom-call | tf_op jit(solution)/shard_map/cond/branch_1_fun/jit(cholesky)/cholesky | solution.py:85
  185.5 9.8 %custom-call.55 = f32[1,128,128]{1,2,0:T(8,128)S(1)} custom-call(f32[1,128,128]{2,1,0:T(8,128)S(1)} %get-tuple-element.130), custom_call_target="InvertDiagBlocksLowerTriangular" | custom-call | tf_op jit(solution)/shard_map/cond/branch_1_fun/jit(cholesky)/cholesky | solution.py:85
  201.7 11.9 %cholesky.27 = f32[128,128]{1,0:T(8,128)S(1)} custom-call(f32[128,128]{1,0:T(8,128)S(1)} %cholesky.227), custom_call_target="Cholesky" | custom-call | tf_op jit(solution)/shard_map/cond/branch_1_fun/jit(cholesky)/cholesky | solution.py:85
  216.2 9.8 %custom-call.56 = f32[1,128,128]{1,2,0:T(8,128)S(1)} custom-call(f32[1,128,128]{2,1,0:T(8,128)S(1)} %get-tuple-element.127), custom_call_target="InvertDiagBlocksLowerTriangular" | custom-call | tf_op jit(solution)/shard_map/cond/branch_1_fun/jit(cholesky)/cholesky | solution.py:85
  229.4 11.7 %cholesky.58 = f32[128,128]{1,0:T(8,128)S(1)} custom-call(f32[128,128]{1,0:T(8,128)S(1)} %cholesky.232), custom_call_target="Cholesky" | custom-call | tf_op jit(solution)/shard_map/cond/branch_1_fun/jit(cholesky)/cholesky | solution.py:85
  243.1 9.8 %custom-call.57 = f32[1,128,128]{1,2,0:T(8,128)S(1)} custom-call(f32[1,128,128]{2,1,0:T(8,128)S(1)} %get-tuple-element.124), custom_call_target="InvertDiagBlocksLowerTriangular" | custom-call | tf_op jit(solution)/shard_map/cond/branch_1_fun/jit(cholesky)/cholesky | solution.py:85
  256.9 11.7 %cholesky.87 = f32[128,128]{1,0:T(8,128)S(1)} custom-call(f32[128,128]{1,0:T(8,128)S(1)} %cholesky.237), custom_call_target="Cholesky" | custom-call | tf_op jit(solution)/shard_map/cond/branch_1_fun/jit(cholesky)/cholesky | solution.py:85
  270.6 9.8 %custom-call.58 = f32[1,128,128]{1,2,0:T(8,128)S(1)} custom-call(f32[1,128,128]{2,1,0:T(8,128)S(1)} %get-tuple-element.121), custom_call_target="InvertDiagBlocksLowerTriangular" | custom-call | tf_op jit(solution)/shard_map/cond/branch_1_fun/jit(cholesky)/cholesky | solution.py:85
  283.9 11.7 %cholesky.116 = f32[128,128]{1,0:T(8,128)S(1)} custom-call(f32[128,128]{1,0:T(8,128)S(1)} %cholesky.242), custom_call_target="Cholesky" | custom-call | tf_op jit(solution)/shard_map/cond/branch_1_fun/jit(cholesky)/cholesky | solution.py:85
  297.6 10.0 %custom-call.59 = f32[1,128,128]{1,2,0:T(8,128)S(1)} custom-call(f32[1,128,128]{2,1,0:T(8,128)S(1)} %get-tuple-element.118), custom_call_target="InvertDiagBlocksLowerTriangular" | custom-call | tf_op jit(solution)/shard_map/cond/branch_1_fun/jit(cholesky)/cholesky | solution.py:85
  310.9 11.7 %cholesky.146 = f32[128,128]{1,0:T(8,128)S(1)} custom-call(f32[128,128]{1,0:T(8,128)S(1)} %cholesky.249), custom_call_target="Cholesky" | custom-call | tf_op jit(solution)/shard_map/cond/branch_1_fun/jit(cholesky)/cholesky | solution.py:85
  324.7 9.8 %custom-call.60 = f32[1,128,128]{1,2,0:T(8,128)S(1)} custom-call(f32[1,128,128]{2,1,0:T(8,128)S(1)} %get-tuple-element.115), custom_call_target="InvertDiagBlocksLowerTriangular" | custom-call | tf_op jit(solution)/shard_map/cond/branch_1_fun/jit(cholesky)/cholesky | solution.py:85
  337.4 12.1 %cholesky.176 = f32[128,128]{1,0:T(8,128)S(1)} custom-call(f32[128,128]{1,0:T(8,128)S(1)} %cholesky.256), custom_call_target="Cholesky" | custom-call | tf_op jit(solution)/shard_map/cond/branch_1_fun/jit(cholesky)/cholesky | solution.py:85
  351.6 9.8 %custom-call.61 = f32[1,128,128]{1,2,0:T(8,128)S(1)} custom-call(f32[1,128,128]{2,1,0:T(8,128)S(1)} %get-tuple-element.112), custom_call_target="InvertDiagBlocksLowerTriangular" | custom-call | tf_op jit(solution)/shard_map/cond/branch_1_fun/jit(cholesky)/cholesky | solution.py:85
  364.0 11.7 %cholesky.204 = f32[128,128]{1,0:T(8,128)S(1)} custom-call(f32[128,128]{1,0:T(8,128)S(1)} %convolution_subtract_fusion.11), custom_call_target="Cholesky" | custom-call | tf_op jit(solution)/shard_map/cond/branch_1_fun/jit(cholesky)/cholesky | solution.py:85
  382.6 24.1 %while.3 = (s32[]{:T(128)}, f32[1024,1024]{1,0:T(8,128)}, s32[8,2]{0,1:T(2,128)S(1)}, f32[8,128,128]{2,1,0:T(8,128)S(1)}, s32[]{:T(128)}) while((s32[]{:T(128)}, f32[1024,1024]{1,0:T(8,128)}, s32[8,2]{0,1:T(2,128)S(1)}, f32[8,128,128]{2,1,0:T(8,128)S(1)}, s32[]{:T(128)}) %tuple.95), condition=%wide.while_cond, body=%wide.while_body.sunk | while | flops 2 | bytes 131189 | solution.py:89
  406.7 78.6 %custom-call.62 = f32[8,128,128]{1,2,0:T(8,128)S(1)} custom-call(f32[8,128,128]{2,1,0:T(8,128)S(1)} %get-tuple-element.27), custom_call_target="InvertDiagBlocksLowerTriangular" | custom-call | tf_op jit(solution)/shard_map/cond/branch_1_fun/jit(_solve_triangular)/triangular_solve | solution.py:89
  485.3 23.3 %select_add_fusion = f32[4,1024,1024]{2,1,0:T(8,128)} fusion(f32[]{:T(128)S(6)} %mul.122, f32[]{:T(128)} %get-tuple-element.4, f32[4,4,1024]{2,0,1:T(4,128)S(1)} %get-tuple-element.64, f32[4,1024]{1,0:T(4,128)S(1)} %get-tuple-element.15), kind=kOutput, calls=%fused_computation.5 | convolution fusion | flops 234881024 | bytes 16859144 | tf_op jit(solution)/shard_map/cond/branch_1_fun/...ka,kb->...ab/dot_general | solution.py:28
  508.6 17.6 %copy.28 = f32[4096,1024]{0,1:T(8,128)} copy(f32[4096,1024]{1,0:T(8,128)} %bitcast.202) | data formatting | bytes 33554432 | tf_op jit(solution)/shard_map/cond/branch_1_fun/reshape | solution.py:90
  581.3 9.3 %convolution_subtract_fusion.1 = f32[128,4096]{1,0:T(8,128)S(1)} fusion(f32[640,4096]{1,0:T(8,128)} %get-tuple-element.96, f32[1024,4096]{1,0:T(8,128)S(1)} %bitcast.199, f32[1024,1024]{1,0:T(8,128)} %get-tuple-element.212), kind=kOutput, calls=%fused_computation.22 | convolution fusion | flops 4027056128 | bytes 15007744 | tf_op jit(solution)/shard_map/cond/branch_1_fun/jit(_solve_triangular)/triangular_solve | solution.py:89
  596.0 9.8 %convolution_subtract_fusion = f32[128,4096]{1,0:T(8,128)S(1)} fusion(f32[768,4096]{1,0:T(8,128)} %get-tuple-element.93, f32[1024,4096]{1,0:T(8,128)S(1)} %bitcast.200, f32[1024,1024]{1,0:T(8,128)} %get-tuple-element.212), kind=kOutput, calls=%fused_computation.21 | convolution fusion | flops 4832362496 | bytes 17170432 | tf_op jit(solution)/shard_map/cond/branch_1_fun/jit(_solve_triangular)/triangular_solve | solution.py:89
  610.3 11.7 %convolution_subtract_fusion.4 = f32[128,4096]{1,0:T(8,128)S(1)} fusion(f32[896,4096]{1,0:T(8,128)} %constant_dynamic-update-slice_fusion.11, f32[1024,4096]{1,0:T(8,128)S(1)} %bitcast.201, f32[1024,1024]{1,0:T(8,128)} %get-tuple-element.212), kind=kOutput, calls=%fused_computation.25 | convolution fusion | flops 5637668864 | bytes 19333120 | tf_op jit(solution)/shard_map/cond/branch_1_fun/jit(_solve_triangular)/triangular_solve | solution.py:89
  624.9 11.9 %copy.38 = bf16[4096,1024]{1,0:T(8,128)(2,1)} copy(bf16[4096,1024]{0,1:T(8,128)(2,1)} %bitcast.26) | data formatting | bytes 16777216 | tf_op jit(solution)/shard_map/cond | solution.py:97
  644.5 123.6 %all-reduce.6.cloned.1.call-done = bf16[4,1024,1024]{2,1,0:T(8,128)(2,1)} async-done(((bf16[4,1024,1024]{2,1,0:T(8,128)(2,1)}), bf16[4,1024,1024]{2,1,0:T(8,128)(2,1)}) %all-reduce.6.cloned.1.call-update) | async-done | bytes 8388624 | tf_op jit(solution)/shard_map/psum | solution.py:14
  772.2 8.4 psum.22
  780.7 76.9 %all-reduce.8.cloned.1.call-done = bf16[1024,1024]{1,0:T(8,128)(2,1)} async-done(((bf16[1024,1024]{1,0:T(8,128)(2,1)}), bf16[1024,1024]{1,0:T(8,128)(2,1)}) %all-reduce.8.cloned.1.call-update) | async-done | bytes 2097168 | tf_op jit(solution)/shard_map/psum | solution.py:14
  899.7 7.8 copy.122
  (161 shorter events, 231.4 us)
Async XLA Ops:
  57.1 14.4 %all-to-all-start = ((s32[32,1,17]{2,1,0:T(1,128)}), s32[32,1,17]{2,1,0:T(1,128)S(1)}, u32[]{:S(2)}, u32[]{:S(2)}) async-start(s32[32,1,17]{2,1,0:T(1,128)} %copy.31), calls=%async_computation | async-start | bytes 32768 | tf_op jit(solution)/shard_map/all_to_all | solution.py:58
  64.4 703.7 %all-reduce.6.cloned.1.call-start = ((), (), s32[]{:S(2)}) async-start(), calls=%async_computation.1 | async-start | bytes 16777216 | tf_op jit(solution)/shard_map/psum | solution.py:14
  154.3 1.9 copy-start.1
  171.7 2.0 copy-start.2
  526.3 11.9 %copy-start = (f32[4096,1024]{0,1:T(8,128)S(1)}, f32[4096,1024]{0,1:T(8,128)}, u32[]{:S(2)}) copy-start(f32[4096,1024]{0,1:T(8,128)} %copy.28) | copy-start | bytes 50331652 | tf_op jit(solution)/shard_map/cond
  644.4 213.2 %all-reduce.8.cloned.1.call-start = ((), (), s32[]{:S(2)}) async-start(), calls=%async_computation.2 | async-start | bytes 4194304 | tf_op jit(solution)/shard_map/psum | solution.py:14
  862.2 6.1 copy-start.3
  862.2 16.3 %slice-start = ((s8[8388608]{0:T(1024)(128)(4,1)}), s8[4194304]{0:T(1024)(128)(4,1)S(1)}, s32[]{:S(2)}) async-start(s8[8388608]{0:T(1024)(128)(4,1)} %bitcast.203), calls=%async_computation.3 | async-start | bytes 8388608
  868.3 10.2 %slice-start.1 = ((s8[8388608]{0:T(1024)(128)(4,1)}), s8[4194304]{0:T(1024)(128)(4,1)S(1)}, s32[]{:S(2)}) async-start(s8[8388608]{0:T(1024)(128)(4,1)} %bitcast.203), calls=%async_computation.4 | async-start | bytes 8388608
Sparse Core Ops, SparseCore 0:
  644.5 123.5 all-reduce.5
  771.4 86.2 all-reduce.7
where the time goes:
time: 926 us; the launch traced here: 915 us
  other arithmetic  284 us (31%)
  waiting for transfers between devices  207 us (22%)
  local copies, waits for them, and re-layouts  174 us (19%)
  matrix products  165 us (18%)
  blocking collectives  54.6 us (6%)
  between operations  16.2 us (2%)
    psum x2, waiting for transfers between devices, from_root(): return lax.psum(kept, axis)  201 us
    another operation x30, other arithmetic, factor_panel(): jnp.linalg.cholesky(cov_tile(panel_left, panel_right, decay_rate, nugget,...  173 us
    another operation x3, other arithmetic, factor_panel(): jax.scipy.linalg.solve_triangular(diag_factor, tiles.reshape(TR_DEV * B,...  83.5 us
    another operation x15, matrix products, factor_panel(): jax.scipy.linalg.solve_triangular(diag_factor, tiles.reshape(TR_DEV * B,...  77.4 us
    dot_general x6, matrix products, cov_tile(): jnp.einsum('...ka,kb->...ab', left, right, precision=lax.Precision.HIGHEST)  51.4 us
    scatter x1, local copies, waits for them, and re-layouts, body(): jnp.full((devices, capacity), -1, jnp.int32).at[home_dev, arrival_rank]  46.5 us
    unnamed x1, blocking collectives  38.2 us
    scatter x1, local copies, waits for them, and re-layouts, body(): row_home = jnp.full((TR_DEV, row_width), -1, jnp.int32).at[tile_index, go...  25.6 us
  transfers between devices with their start and end apart: 3, of which 3 were waited for; matrix products, arithmetic and copies ran while one was open for 0% of the time, Pallas kernels for 0%

commit v1 on v0

--- a/solution.py
+++ b/solution.py
@@ -9,9 +9,15 @@
 SLAB_DEV = 1
 
 
+def summed_here(x, mesh_axis):
+    pieces = lax.all_gather(x, mesh_axis, axis=0, tiled=False)
+    summed = pieces.sum(axis=0)
+    return summed
+
+
 def from_root(value, axis, source):
     kept = jnp.where(lax.axis_index(axis) == source, value, 0).astype(value.dtype)
-    return lax.psum(kept, axis)
+    return summed_here(kept, axis)
 
 
 def site_features(codes):

time: 926 us -> 1210 us (1.31)
  waiting for transfers between devices: 207 us -> 441 us
  other arithmetic: 284 us -> 322 us
    all_gather x0 -> x2, waiting for transfers between devices: none -> 435 us  [summed_here(): pieces = lax.all_gather(x, mesh_axis, axis=0, tiled=False)]
    psum x2 -> x0, waiting for transfers between devices: 201 us -> none  [from_root(): return lax.psum(kept, axis)]
    reduce_sum x0 -> x3, other arithmetic: none -> 32.6 us  [summed_here(): summed = pieces.sum(axis=0)]
    all_gather x0 -> x1, blocking collectives: none -> 13.7 us  [summed_here(): pieces = lax.all_gather(x, mesh_axis, axis=0, tiled=False)]
where the time goes in v1:
time: 1210 us; the launch traced here: 1200 us
  waiting for transfers between devices  441 us (36%)
  other arithmetic  322 us (27%)
  local copies, waits for them, and re-layouts  185 us (15%)
  matrix products  165 us (14%)
  blocking collectives  59.9 us (5%)
  between operations  16 us (1%)
    all_gather x2, waiting for transfers between devices, summed_here(): pieces = lax.all_gather(x, mesh_axis, axis=0, tiled=False)  435 us
    another operation x30, other arithmetic, factor_panel(): jnp.linalg.cholesky(cov_tile(panel_left, panel_right, decay_rate, nugget,...  172 us
    another operation x3, other arithmetic, factor_panel(): jax.scipy.linalg.solve_triangular(diag_factor, tiles.reshape(TR_DEV * B,...  83.5 us
    another operation x15, matrix products, factor_panel(): jax.scipy.linalg.solve_triangular(diag_factor, tiles.reshape(TR_DEV * B,...  77.4 us
    dot_general x6, matrix products, cov_tile(): jnp.einsum('...ka,kb->...ab', left, right, precision=lax.Precision.HIGHEST)  51.3 us
    scatter x1, local copies, waits for them, and re-layouts, body(): jnp.full((devices, capacity), -1, jnp.int32).at[home_dev, arrival_rank]  46.5 us
    unnamed x1, blocking collectives  38.2 us
    reduce_sum x3, other arithmetic, summed_here(): summed = pieces.sum(axis=0)  32.6 us
  transfers between devices with their start and end apart: 3, of which 3 were waited for; matrix products, arithmetic and copies ran while one was open for 0% of the time, Pallas kernels for 0%

profile of v1, /device:TPU:0, one launch (start us, length us, event | category | flops | bytes accessed | tf_op | source)
XLA Modules:
  0.0 1203.2 jit_solution(5827223571942501718)
XLA Ops:
  9.8 46.5 %scatter_fusion = s32[32,17]{0,1:T(8,128)S(1)} fusion(s32[32,17]{0,1:T(8,128)S(1)} %broadcast_in_dim.87, s32[544]{0:T(1024)S(1)} %fusion.112, s32[544]{0:T(1024)} %param.5), kind=kCustom, calls=%fused_computation | custom fusion | bytes 10880 | tf_op jit(solution)/shard_map/scatter | solution.py:63
  73.1 25.6 %scatter_fusion.1 = s32[4,128]{1,0:T(4,128)S(1)} fusion(s32[4,128]{1,0:T(4,128)S(1)} %broadcast_in_dim.89, s32[544]{0:T(1024)S(1)} %get-tuple-element.75, s32[544]{0:T(1024)S(1)} %reshape.1176), kind=kCustom, calls=%fused_computation.2 | custom fusion | bytes 10880 | tf_op jit(solution)/shard_map/scatter | solution.py:76
  111.4 38.2 %all-reduce.2 = s32[1024]{0:T(1024)S(1)} all-reduce(s32[1024]{0:T(1024)S(1)} %dynamic-update-slice.49), channel_id=1, replica_groups=mesh['prow'=4,'pcol'=8] {'prow','pcol'}, use_global_device_ids=true, to_apply=%add.2 | all-reduce | flops 1024 | bytes 8192
  150.1 485.5 %conditional.1 = (bf16[4,1024,1024]{2,1,0:T(8,128)(2,1)}) conditional(s32[]{:T(128)} %convert_element_type.130, () %tuple.14, (f32[]{:T(128)}, f32[4,1024]{1,0:T(4,128)S(1)}, f32[4,1024]{1,0:T(4,128)S(1)}, f32[]{:T(128)}, f32[4,4,1024]{2,0,1:T(4,128)S(1)}) %tuple.15), branch_computations={%region_6.7_spmd, %region_7.24_spmd} | conditional | flops 32137316352 | bytes 414441856 | solution.py:103
  173.7 11.7 cholesky.5
  185.5 9.8 custom-call.55
  201.7 11.9 cholesky.27
  216.1 9.8 custom-call.56
  229.3 11.7 cholesky.58
  242.9 9.8 custom-call.57
  256.7 11.7 cholesky.87
  270.3 9.8 custom-call.58
  283.6 11.7 cholesky.116
  297.2 10.0 custom-call.59
  310.5 11.7 cholesky.146
  324.1 9.8 custom-call.60
  336.9 12.1 %cholesky.176 = f32[128,128]{1,0:T(8,128)S(1)} custom-call(f32[128,128]{1,0:T(8,128)S(1)} %cholesky.256), custom_call_target="Cholesky" | custom-call | tf_op jit(solution)/shard_map/cond/branch_1_fun/jit(cholesky)/cholesky | solution.py:91
  351.0 9.8 custom-call.61
  363.4 11.7 cholesky.204
  381.9 23.2 %while.3 = (s32[]{:T(128)}, f32[1024,1024]{1,0:T(8,128)}, s32[8,2]{0,1:T(2,128)S(1)}, f32[8,128,128]{2,1,0:T(8,128)S(1)}, s32[]{:T(128)}) while((s32[]{:T(128)}, f32[1024,1024]{1,0:T(8,128)}, s32[8,2]{0,1:T(2,128)S(1)}, f32[8,128,128]{2,1,0:T(8,128)S(1)}, s32[]{:T(128)}) %tuple.98), condition=%wide.while_cond, body=%wide.while_body.sunk | while | flops 2 | bytes 131189 | solution.py:95
  405.2 78.6 %custom-call.62 = f32[8,128,128]{1,2,0:T(8,128)S(1)} custom-call(f32[8,128,128]{2,1,0:T(8,128)S(1)} %get-tuple-element.27), custom_call_target="InvertDiagBlocksLowerTriangular" | custom-call | tf_op jit(solution)/shard_map/cond/branch_1_fun/jit(_solve_triangular)/triangular_solve | solution.py:95
  483.8 23.3 %select_add_fusion = f32[4,1024,1024]{2,1,0:T(8,128)} fusion(f32[]{:T(128)S(6)} %mul.158, f32[]{:T(128)} %get-tuple-element.4, f32[4,4,1024]{2,0,1:T(4,128)S(1)} %get-tuple-element.71, f32[4,1024]{1,0:T(4,128)S(1)} %get-tuple-element.15), kind=kOutput, calls=%fused_computation.5 | convolution fusion | flops 234881024 | bytes 16859144 | tf_op jit(solution)/shard_map/cond/branch_1_fun/...ka,kb->...ab/dot_general | solution.py:34
  507.1 17.6 %copy.37 = f32[4096,1024]{0,1:T(8,128)} copy(f32[4096,1024]{1,0:T(8,128)} %bitcast.198) | data formatting | bytes 33554432 | tf_op jit(solution)/shard_map/cond/branch_1_fun/reshape | solution.py:96
  579.7 9.3 convolution_subtract_fusion.1
  594.5 9.9 convolution_subtract_fusion
  608.8 11.7 convolution_subtract_fusion.4
  623.4 11.9 copy.54
  643.0 300.1 %all-gather.7.cloned.1.call-done = bf16[32,1024,1024]{2,1,0:T(8,128)(2,1)} async-done(((bf16[4,1024,1024]{2,1,0:T(8,128)(2,1)}), bf16[32,1024,1024]{2,1,0:T(8,128)(2,1)}) %all-gather.7.cloned.1.call-update) | async-done | bytes 67108880 | tf_op jit(solution)/shard_map/all_gather | solution.py:13
  943.1 26.1 %reduce_sum.45 = bf16[4,1024,1024]{2,1,0:T(8,128)(2,1)} reduce(bf16[8,4,1024,1024]{3,2,1,0:T(8,128)(2,1)} %bitcast.33, bf16[]{:T(256)} %constant.564.clone.1), dimensions={0}, to_apply=%region_24.25 | reduce | flops 29360128 | bytes 75497472 | tf_op jit(solution)/shard_map/reduce_sum | solution.py:14
  987.7 10.6 copy.47
  999.2 13.7 %all-gather.3 = s32[4,1,1024]{2,1,0:T(1,128)S(1)} all-gather(s32[1,1,1024]{2,1,0:T(1,128)S(1)} %fusion.98), channel_id=3, replica_groups=mesh['prow'=4,'pcol'=8] {'prow'}, dimensions={0}, use_global_device_ids=true | all-gather | bytes 20480 | tf_op jit(solution)/shard_map/all_gather | solution.py:13
  1013.0 135.1 %all-gather.9.cloned.1.call-done = bf16[4,1024,1024]{2,1,0:T(8,128)(2,1)} async-done(((bf16[1,1024,1024]{2,1,0:T(8,128)(2,1)}), bf16[4,1024,1024]{2,1,0:T(8,128)(2,1)}) %all-gather.9.cloned.1.call-update) | async-done | bytes 8388624 | tf_op jit(solution)/shard_map/all_gather | solution.py:13
  (164 shorter events, 259.6 us)
Async XLA Ops:
  57.1 14.4 %all-to-all-start = ((s32[32,1,17]{2,1,0:T(1,128)}), s32[32,1,17]{2,1,0:T(1,128)S(1)}, u32[]{:S(2)}, u32[]{:S(2)}) async-start(s32[32,1,17]{2,1,0:T(1,128)} %copy.40), calls=%async_computation | async-start | bytes 32768 | tf_op jit(solution)/shard_map/all_to_all | solution.py:64
  64.4 878.7 %all-gather.7.cloned.1.call-start = ((), (), s32[]{:S(2)}) async-start(), calls=%async_computation.1 | async-start | bytes 75497472 | tf_op jit(solution)/shard_map/all_gather | solution.py:13
  154.3 1.9 copy-start.1
  171.7 2.0 copy-start.2
  524.7 11.9 copy-start
  642.9 505.1 %all-gather.9.cloned.1.call-start = ((), (), s32[]{:S(2)}) async-start(), calls=%async_computation.2 | async-start | bytes 10485760 | tf_op jit(solution)/shard_map/all_gather | solution.py:13
  1154.6 8.3 slice-start
  1158.7 4.1 slice-start.1
Sparse Core Ops, SparseCore 0:
  643.0 300.0 all-gather.6
  998.4 149.6 all-gather.8
